TPU v7x, 32 devices: a whole 2x2x4 slice. The times are simulated.
32 devices in a mesh: set: 4 (over z), path: 2 (over y), tm: 4 (over x, core).
Axes of the slice: x: 2, y: 2, z: 4, core: 2. Of those that a mesh axis runs over, the one named last changes fastest.
Arguments:
- normals: bfloat16 [1024, 2048], P(('set', 'path'), 'tm'), parts along dimension 0, may hold values from -6 to 6
- orth_normals: bfloat16 [1024, 2048], P(('set', 'path'), 'tm'), parts along dimension 0, may hold values from -6 to 6
- forward_var: float32 [8192], P(('set', 'tm')), parts along dimension 0, may hold values from 0.02 to 0.2
- hurst: float32 [4], P('set'), parts along dimension 0, may hold values from 0.05 to 0.25
- eta: float32 [4], P('set'), parts along dimension 0, may hold values from 1 to 2.5
- rho: float32 [4], P('set'), parts along dimension 0, may hold values from -0.95 to -0.5
- strike_index: int32 [1024], P('set'), parts along dimension 0, may hold values from 0 to 10
- maturity_index: int32 [1024], P('set'), parts along dimension 0, may hold values from 0 to 2047
Outputs:
- log_price: float32 [1024, 2048], P(('set', 'path'), 'tm'), parts along dimension 0
- prices: float32 [1024], P('set'), parts along dimension 0
There are 4 independent parts, one for each index of `set`. A program takes and returns all parts, laid end to end along the dimension named above; each array names one. Nothing has to cross between parts.
All inputs are finite; a program needn't handle non-finite values.
Results may differ from a plain program's by a relative error of at most 0.0047.
The roundings to bfloat16 on the way count: a program that leaves them out, or rounds other values in their place, can miss the bound.
Values may be sent and summed in bfloat16 or wider, within the bound.
No kernel may reach another device: no remote copies, remote signals or barrier semaphores. Data moves between devices by JAX's collectives and lax.ppermute only.
A program may use at most 64 MiB of HBM per device.

v0:
```python
import math
import jax
import jax.numpy as jnp
from jax import lax
from jax.sharding import PartitionSpec as P

STRIKES = 11
horizon = 2.0


def entering(value, axis, join, neutral):
    count, mine = (lax.axis_size(axis), lax.axis_index(axis))
    pieces = lax.all_gather(value, axis)
    total = jnp.full_like(value, 0) + jnp.asarray(neutral, value.dtype)

    def hop(position, total):
        longer = join(total, pieces[position])
        return jnp.where(position < mine, longer, total)

    return lax.fori_loop(0, count - 1, hop, total)


def increment_block(row_count, col_start, col_count, steps):
    rows = jnp.arange(row_count, dtype=jnp.int32)
    cols = col_start + jnp.arange(col_count, dtype=jnp.int32)
    period = 4 * (2 * steps + 1)
    phase = (2 * rows[:, None] + 1) * (2 * cols[None, :] + 1) % period
    step = horizon / steps
    scale = math.sqrt(step) * 2.0 / math.sqrt(2 * steps + 1)
    return (scale * jnp.cos(math.pi * phase.astype(jnp.float32) / (2 * (2 * steps + 1)))).astype(
        jnp.bfloat16
    )


def kernel_block(hurst_value, step, lag):
    expo = hurst_value - 0.5
    safe = jnp.maximum(lag, 1).astype(jnp.float32)
    inner = -jnp.expm1((expo + 1.0) * jnp.log1p(-1.0 / safe))
    log_b = ((expo + 1.0) * jnp.log(safe) + jnp.log(inner) - jnp.log(expo + 1.0)) / expo
    values = jnp.sqrt(2.0 * hurst_value) * jnp.exp(expo * (log_b + math.log(step)))
    return jnp.where(lag >= 1, values, 0.0).astype(jnp.bfloat16)


def prefix_sum(values):
    row_count = values.shape[0]
    length = values.shape[1]
    width_block = 512
    blocks = length // width_block
    shaped = values.reshape(row_count, blocks, width_block)
    ar_block = jnp.arange(width_block, dtype=jnp.int32)
    upper = (ar_block[:, None] <= ar_block[None, :]).astype(jnp.float32)
    inner = jnp.einsum("rbs,si->rbi", shaped, upper, precision=lax.Precision.HIGHEST)
    totals = inner[:, :, -1]
    before = jnp.cumsum(totals, axis=1) - totals
    return (inner + before[:, :, None]).reshape(row_count, length)


def pick_columns(log_price, first_step, maturity_index):
    count = log_price.shape[1]
    columns = first_step + jnp.arange(count, dtype=jnp.int32)
    onehot = (columns[:, None] == maturity_index[None, :]).astype(jnp.float32)
    inside = jnp.sum(onehot, axis=0) > 0.5
    picked = jnp.dot(
        log_price, onehot, precision=lax.Precision.HIGHEST, preferred_element_type=jnp.float32
    )
    return (picked, inside)


def increments(dw, orth_rows, volterra, curve, first_step, step, hurst_value, eta_value, rho_value):
    count = dw.shape[1]
    times = (first_step + jnp.arange(count, dtype=jnp.int32)).astype(jnp.float32) * step
    variance = curve[None, :] * jnp.exp(
        eta_value * volterra - 0.5 * eta_value * eta_value * (times ** (2.0 * hurst_value))[None, :]
    )
    noise = rho_value * dw.astype(jnp.float32) + jnp.sqrt(1.0 - rho_value * rho_value) * math.sqrt(
        step
    ) * orth_rows.astype(jnp.float32)
    return jnp.sqrt(variance) * noise - 0.5 * variance * step


def add_pair(earlier, later):
    return earlier + later


def local_tail(
    dw,
    orth_normals,
    volterra,
    forward_var,
    offset,
    step,
    hurst_value,
    eta_value,
    rho_value,
    strikes,
    maturity_index,
):
    increment = increments(
        dw, orth_normals, volterra, forward_var, offset, step, hurst_value, eta_value, rho_value
    )
    partial_log = prefix_sum(increment)
    totals = partial_log[:, -1]
    before = entering(totals, "tm", add_pair, jnp.zeros_like(totals))
    log_price = partial_log + before[:, None]
    picked, inside = pick_columns(log_price, offset, maturity_index)
    payoff = jnp.where(inside[None, :], jnp.maximum(jnp.exp(picked) - strikes[None, :], 0.0), 0.0)
    return (log_price, jnp.sum(payoff, axis=0))


def on_device(normals, orth_normals, forward_var, hurst, eta, rho, strike_index, maturity_index):
    path_rows = normals.shape[0]
    width = normals.shape[1]
    tm_count = lax.axis_size("tm")
    steps = width * tm_count
    step = horizon / steps
    block = lax.axis_index("tm")
    offset = block * width
    hurst_value = hurst[0]
    eta_value = eta[0]
    rho_value = rho[0]
    strikes = 0.5 + strike_index.astype(jnp.float32) / (STRIKES - 1)
    ar_width = jnp.arange(width, dtype=jnp.int32)
    piece = lax.all_gather(normals, "tm", axis=1, tiled=True)
    table = increment_block(piece.shape[1], offset, width, steps)
    dw_sum = jnp.dot(piece, table, preferred_element_type=jnp.float32)
    dw = dw_sum.astype(jnp.bfloat16)
    piece = lax.all_gather(dw, "tm", axis=1, tiled=True)
    sources = jnp.arange(piece.shape[1], dtype=jnp.int32)
    lag = (offset + ar_width)[None, :] - sources[:, None]
    volterra = jnp.dot(
        piece, kernel_block(hurst_value, step, lag), preferred_element_type=jnp.float32
    )
    log_price, partial_value = local_tail(
        dw,
        orth_normals,
        volterra,
        forward_var,
        offset,
        step,
        hurst_value,
        eta_value,
        rho_value,
        strikes,
        maturity_index,
    )
    total_paths = path_rows * lax.axis_size("path")
    prices = lax.psum(partial_value, ("path", "tm")) / total_paths
    return (log_price, prices)


def solution(mesh):
    in_specs = (
        P(("set", "path"), "tm"),
        P(("set", "path"), "tm"),
        P(("set", "tm")),
        P("set"),
        P("set"),
        P("set"),
        P("set"),
        P("set"),
    )
    out_specs = (P(("set", "path"), "tm"), P("set"))
    return jax.shard_map(
        on_device, mesh=mesh, in_specs=in_specs, out_specs=out_specs, check_vma=False
    )
```

profile of v0, /device:TPU:0, one launch (start us, length us, event | category | flops | bytes accessed | tf_op | source)
XLA Modules:
  0.0 64.6 jit_solution(15451301381993555974)
XLA Ops:
  2.0 8.8 %all_gather.9 = bf16[128,2048]{1,0:T(8,128)(2,1)S(1)} all-gather(bf16[128,512]{1,0:T(8,128)(2,1)} %param.10), channel_id=1, replica_groups=mesh['set'=4,'path'=2,'tm'=4] {'tm'}, dimensions={1}, use_global_device_ids=true | all-gather | bytes 655360 | tf_op jit(solution)/shard_map/all_gather | solution.py:123
  10.8 16.3 %fusion.22 = bf16[128,512]{0,1:T(8,128)(2,1)S(1)} fusion(bf16[128,2048]{1,0:T(8,128)(2,1)S(1)} %all_gather.9, s32[512]{0:T(512)S(1)} %multiply_add_fusion.1, s32[2048]{0:T(1024)S(1)} %multiply_add_fusion), kind=kOutput, calls=%fused_computation.26 | convolution fusion | flops 280035328 | bytes 665600 | tf_op jit(solution)/shard_map/dot_general | solution.py:125
  27.2 0.0 copy-start.4
  27.2 7.3 %all_gather.10 = bf16[128,2048]{0,1:T(8,128)(2,1)S(1)} all-gather(bf16[128,512]{0,1:T(8,128)(2,1)S(1)} %fusion.22), channel_id=1, replica_groups=mesh['set'=4,'path'=2,'tm'=4] {'tm'}, dimensions={1}, use_global_device_ids=true | all-gather | bytes 655360 | tf_op jit(solution)/shard_map/all_gather | solution.py:127
  34.6 0.0 copy-done.4
  34.6 0.0 copy-start.1
  34.6 6.8 %fusion.15 = f32[128,512]{0,1:T(8,128)S(1)} fusion(bf16[128,2048]{0,1:T(8,128)(2,1)S(1)} %all_gather.10, f32[]{:T(128)S(6)} %log.11, f32[]{:T(128)} %bitcast.4, f32[]{:T(128)} %bitcast.3, f32[]{:T(128)S(6)} %sqrt.9, s32[512]{0:T(512)S(1)} %iota_add_fusion, f32[512]{0:T(512)S(1)} %power_multiply_fusion, f32[]{:T(128)} %bitcast.16, f32[512]{0:T(512)S(1)} %copy-done.4), kind=kOutput, calls=%fused_computation.20 | convolution fusion | flops 285409280 | bytes 792596 | tf_op jit(solution)/shard_map/dot_general | solution.py:130
  42.0 0.0 copy-done.1
  42.0 0.1 copy.15
  42.2 0.5 fusion.26
  42.7 0.2 fusion.43
  42.9 0.1 broadcast_add_fusion.1
  43.0 0.1 slice.9
  43.1 5.9 %all-gather = f32[512,1]{1,0:T(8,128)S(1)} all-gather(f32[128,1]{1,0:T(8,128)S(1)} %slice.9), channel_id=2, replica_groups=mesh['set'=4,'path'=2,'tm'=4] {'tm'}, dimensions={0}, use_global_device_ids=true | all-gather | bytes 2560 | tf_op jit(solution)/shard_map/all_gather | solution.py:13
  48.9 0.0 copy-start.3
  48.9 0.0 copy-start.2
  48.9 0.1 reduce.1
  49.1 0.1 while.14
  49.2 0.1 broadcast_add_fusion
  49.3 0.3 copy-done.3
  49.6 0.0 copy-start
  49.6 0.1 fusion.28
  49.8 0.0 copy-done.2
  49.8 0.4 fusion.25
  50.2 13.8 %psum.7 = f32[256]{0:T(256)S(1)} all-reduce(f32[256]{0:T(256)S(1)} %fusion.25), channel_id=1, replica_groups=mesh['set'=4,'path'=2,'tm'=4] {'path','tm'}, use_global_device_ids=true, to_apply=%region_4.5 | all-reduce | flops 256 | bytes 2048 | tf_op jit(solution)/shard_map/psum | solution.py:147
  64.0 0.6 broadcast_multiply_fusion
  64.6 0.0 copy-done
  (10 shorter events, 0.1 us)
Async XLA Ops:
  27.2 7.4 %copy-start.4 = (f32[512]{0:T(512)S(1)}, f32[512]{0:T(512)}, u32[]{:S(2)}) copy-start(f32[512]{0:T(512)} %param.12) | copy-start | bytes 6148
  34.6 7.5 %copy-start.1 = (bf16[128,512]{1,0:T(8,128)(2,1)S(1)}, bf16[128,512]{1,0:T(8,128)(2,1)}, u32[]{:S(2)}) copy-start(bf16[128,512]{1,0:T(8,128)(2,1)} %param.11) | copy-start | bytes 393220
  48.9 0.7 %copy-start.3 = (s32[256]{0:T(256)S(1)}, s32[256]{0:T(256)}, u32[]{:S(2)}) copy-start(s32[256]{0:T(256)} %param.17) | copy-start | bytes 3076
  48.9 0.8 %copy-start.2 = (s32[256]{0:T(256)S(1)}, s32[256]{0:T(256)}, u32[]{:S(2)}) copy-start(s32[256]{0:T(256)} %param.16) | copy-start | bytes 3076
  49.6 15.0 %copy-start = (f32[128,512]{1,0:T(8,128)}, f32[128,512]{1,0:T(8,128)S(1)}, u32[]{:S(2)}) copy-start(f32[128,512]{1,0:T(8,128)S(1)} %broadcast_add_fusion) | copy-start | bytes 786436
where the time goes:
time: 64.8 us; the launch traced here: 64.6 us
  blocking collectives  35.8 us (55%)
  matrix products  24 us (37%)
  between operations  2.85 us (4%)
  other arithmetic  1.33 us (2%)
    dot_general x1, matrix products, on_device(): dw_sum = jnp.dot(piece, table, preferred_element_type=jnp.float32)  16.3 us
    psum x1, blocking collectives, on_device(): prices = lax.psum(partial_value, ('path', 'tm')) / total_paths  13.8 us
    all_gather x1, blocking collectives, on_device(): piece = lax.all_gather(normals, 'tm', axis=1, tiled=True)  8.83 us
    all_gather x1, blocking collectives, on_device(): piece = lax.all_gather(dw, 'tm', axis=1, tiled=True)  7.29 us
    dot_general x1, matrix products, on_device(): jnp.dot(piece, kernel_block(hurst_value, step, lag), preferred_element_ty...  6.75 us
    all_gather x1, blocking collectives, entering(): pieces = lax.all_gather(value, axis)  5.86 us

commit v1 on v0

--- a/solution.py
+++ b/solution.py
@@ -144,7 +144,7 @@
         maturity_index,
     )
     total_paths = path_rows * lax.axis_size("path")
-    prices = lax.psum(partial_value, ("path", "tm")) / total_paths
+    prices = jnp.sum(lax.all_gather(partial_value, ("path", "tm")), axis=0) / total_paths
     return (log_price, prices)
 
 

time: 64.8 us -> 59.9 us (0.924)
  blocking collectives: 35.8 us -> 30.9 us
    psum x1 -> x0, blocking collectives: 13.8 us -> none  [on_device(): prices = lax.psum(partial_value, ('path', 'tm')) / total_paths]
    all_gather x0 -> x1, blocking collectives: none -> 8.91 us  [on_device(): lax.all_gather(partial_value, ('path', 'tm'))]
where the time goes in v1:
time: 59.9 us; the launch traced here: 59.7 us
  blocking collectives  30.9 us (52%)
  matrix products  24 us (40%)
  between operations  2.85 us (5%)
  other arithmetic  1.35 us (2%)
    dot_general x1, matrix products, on_device(): dw_sum = jnp.dot(piece, table, preferred_element_type=jnp.float32)  16.3 us
    all_gather x1, blocking collectives, on_device(): lax.all_gather(partial_value, ('path', 'tm'))  8.91 us
    all_gather x1, blocking collectives, on_device(): piece = lax.all_gather(normals, 'tm', axis=1, tiled=True)  8.83 us
    all_gather x1, blocking collectives, on_device(): piece = lax.all_gather(dw, 'tm', axis=1, tiled=True)  7.29 us
    dot_general x1, matrix products, on_device(): jnp.dot(piece, kernel_block(hurst_value, step, lag), preferred_element_ty...  6.75 us
    all_gather x1, blocking collectives, entering(): pieces = lax.all_gather(value, axis)  5.86 us

profile of v1, /device:TPU:0, one launch (start us, length us, event | category | flops | bytes accessed | tf_op | source)
XLA Modules:
  0.0 59.7 jit_solution(3155088062520898032)
XLA Ops:
  2.0 8.8 %all_gather.15 = bf16[128,2048]{1,0:T(8,128)(2,1)S(1)} all-gather(bf16[128,512]{1,0:T(8,128)(2,1)} %param.10), channel_id=1, replica_groups=mesh['set'=4,'path'=2,'tm'=4] {'tm'}, dimensions={1}, use_global_device_ids=true | all-gather | bytes 655360 | tf_op jit(solution)/shard_map/all_gather | solution.py:123
  10.8 16.3 %fusion.22 = bf16[128,512]{0,1:T(8,128)(2,1)S(1)} fusion(bf16[128,2048]{1,0:T(8,128)(2,1)S(1)} %all_gather.15, s32[512]{0:T(512)S(1)} %multiply_add_fusion.1, s32[2048]{0:T(1024)S(1)} %multiply_add_fusion), kind=kOutput, calls=%fused_computation.26 | convolution fusion | flops 280035328 | bytes 665600 | tf_op jit(solution)/shard_map/dot_general | solution.py:125
  27.2 0.0 copy-start.4
  27.2 7.3 %all_gather.16 = bf16[128,2048]{0,1:T(8,128)(2,1)S(1)} all-gather(bf16[128,512]{0,1:T(8,128)(2,1)S(1)} %fusion.22), channel_id=1, replica_groups=mesh['set'=4,'path'=2,'tm'=4] {'tm'}, dimensions={1}, use_global_device_ids=true | all-gather | bytes 655360 | tf_op jit(solution)/shard_map/all_gather | solution.py:127
  34.6 0.0 copy-done.4
  34.6 0.0 copy-start.1
  34.6 6.8 %fusion.15 = f32[128,512]{0,1:T(8,128)S(1)} fusion(bf16[128,2048]{0,1:T(8,128)(2,1)S(1)} %all_gather.16, f32[]{:T(128)S(6)} %log.11, f32[]{:T(128)} %bitcast.4, f32[]{:T(128)} %bitcast.3, f32[]{:T(128)S(6)} %sqrt.9, s32[512]{0:T(512)S(1)} %iota_add_fusion, f32[512]{0:T(512)S(1)} %power_multiply_fusion, f32[]{:T(128)} %bitcast.17, f32[512]{0:T(512)S(1)} %copy-done.4), kind=kOutput, calls=%fused_computation.20 | convolution fusion | flops 285409280 | bytes 792596 | tf_op jit(solution)/shard_map/dot_general | solution.py:130
  42.0 0.0 copy-done.1
  42.0 0.1 copy.17
  42.2 0.5 fusion.26
  42.7 0.2 fusion.43
  42.9 0.1 broadcast_add_fusion.1
  43.0 0.1 slice.9
  43.1 5.9 %all-gather = f32[512,1]{1,0:T(8,128)S(1)} all-gather(f32[128,1]{1,0:T(8,128)S(1)} %slice.9), channel_id=2, replica_groups=mesh['set'=4,'path'=2,'tm'=4] {'tm'}, dimensions={0}, use_global_device_ids=true | all-gather | bytes 2560 | tf_op jit(solution)/shard_map/all_gather | solution.py:13
  48.9 0.0 copy-start.3
  48.9 0.0 copy-start.2
  48.9 0.1 reduce.2
  49.1 0.1 while.14
  49.2 0.1 broadcast_add_fusion
  49.3 0.3 copy-done.3
  49.6 0.0 copy-start
  49.6 0.1 fusion.28
  49.8 0.0 copy-done.2
  49.8 0.4 fusion.25
  50.2 8.9 %all-gather.2 = f32[8,1,256]{2,1,0:T(1,128)S(1)} all-gather(f32[1,1,256]{2,1,0:T(1,128)S(1)} %bitcast.25), channel_id=3, replica_groups=mesh['set'=4,'path'=2,'tm'=4] {'path','tm'}, dimensions={0}, use_global_device_ids=true | all-gather | bytes 9216 | tf_op jit(solution)/shard_map/all_gather | solution.py:147
  59.1 0.6 broadcast_multiply_fusion
  59.7 0.0 copy-done
  (11 shorter events, 0.1 us)
Async XLA Ops:
  27.2 7.4 %copy-start.4 = (f32[512]{0:T(512)S(1)}, f32[512]{0:T(512)}, u32[]{:S(2)}) copy-start(f32[512]{0:T(512)} %param.12) | copy-start | bytes 6148
  34.6 7.5 %copy-start.1 = (bf16[128,512]{1,0:T(8,128)(2,1)S(1)}, bf16[128,512]{1,0:T(8,128)(2,1)}, u32[]{:S(2)}) copy-start(bf16[128,512]{1,0:T(8,128)(2,1)} %param.11) | copy-start | bytes 393220
  48.9 0.7 %copy-start.3 = (s32[256]{0:T(256)S(1)}, s32[256]{0:T(256)}, u32[]{:S(2)}) copy-start(s32[256]{0:T(256)} %param.17) | copy-start | bytes 3076
  48.9 0.8 %copy-start.2 = (s32[256]{0:T(256)S(1)}, s32[256]{0:T(256)}, u32[]{:S(2)}) copy-start(s32[256]{0:T(256)} %param.16) | copy-start | bytes 3076
  49.6 10.1 %copy-start = (f32[128,512]{1,0:T(8,128)}, f32[128,512]{1,0:T(8,128)S(1)}, u32[]{:S(2)}) copy-start(f32[128,512]{1,0:T(8,128)S(1)} %broadcast_add_fusion) | copy-start | bytes 786436
